TPU v7x, 32 devices: a whole 2x2x4 slice. The times are simulated.
32 devices in a mesh: pipe: 2 (over core), ctx: 16 (over z, y, x).
Axes of the slice: x: 2, y: 2, z: 4, core: 2. Of those that a mesh axis runs over, the one named last changes fastest.
Arguments:
- arriving: bfloat16 [2, 4096, 2048], P('pipe', None, 'ctx'), may hold values from -6 to 6
- input_gate: bfloat16 [2, 4096, 2048], P('pipe', None, 'ctx'), may hold values from -6 to 6
- input_inner: bfloat16 [2, 4096, 2048], P('pipe', None, 'ctx'), may hold values from -6 to 6
- values: bfloat16 [2, 4096, 2048], P('pipe', None, 'ctx'), may hold values from -6 to 6
- conv_out: bfloat16 [2, 4096, 2048], P('pipe', None, 'ctx'), may hold values from -6 to 6
- filters: bfloat16 [2, 4096, 2048], P('pipe', None, 'ctx'), may hold values from -1 to 1
- bias: float32 [2, 4096], P('pipe'), may hold values from 0.5 to 1.5
Outputs:
- d_gate: bfloat16 [2, 4096, 2048], P('pipe', None, 'ctx')
- inner_gradient: bfloat16 [2, 4096, 2048], P('pipe', None, 'ctx')
- d_values: bfloat16 [2, 4096, 2048], P('pipe', None, 'ctx')
- d_filters: float32 [2, 4096, 2048], P('pipe', None, 'ctx')
All inputs are finite; a program needn't handle non-finite values.
Results may differ from a plain program's by a relative error of at most 0.011.
Values may be sent and summed in bfloat16 or wider, within the bound.
A program may use at most 128 MiB of HBM per device.

v0:
```python
import functools
import math

import jax
import jax.numpy as jnp
from jax import lax
from jax.experimental import pallas as pl
from jax.experimental.pallas import tpu as pltpu
from jax.sharding import PartitionSpec as P


def plus(a, b):
    return b if a is None else a if b is None else a + b


def minus(a, b):
    return a if b is None else -b if a is None else a - b


def turn(a, b, k, n):
    k = k % n
    if k == 0:
        return a, b
    if 4 * k == n:
        return b, minus(None, a)
    if 4 * k == 3 * n:
        return minus(None, b), a
    c, s = math.cos(2 * math.pi * k / n), math.sin(2 * math.pi * k / n)

    def scaled(v, f):
        return None if v is None else v * f

    if 8 * k == n:
        return scaled(plus(a, b), c), scaled(minus(b, a), c)
    return plus(scaled(a, c), scaled(b, s)), minus(scaled(b, c), scaled(a, s))


def real_dft(x, n):
    if n == 2:
        return [(x[0], None), (x[0], None)]
    even, odd = real_dft(x[0::2], n // 2), real_dft(x[1::2], n // 2)
    out = [None] * (n // 2 + 1)
    for k in range(n // 4 + 1):
        er, ei = even[k]
        tr, ti = turn(*odd[k], k, n)
        if 4 * k == n:
            out[k] = (plus(er, tr), plus(ei, ti))
        else:
            out[k] = (plus(er, tr), plus(ei, ti))
            out[n // 2 - k] = (minus(er, tr), minus(ti, ei))
    return out


def real_inverse(spec, n):
    if n == 2:
        return [plus(spec[0][0], spec[1][0])]
    even, odd = [], []
    for k in range(n // 4 + 1):
        xr, xi = spec[k]
        if 4 * k == n:
            even.append((xr + xr, None))
            odd.append((minus(None, None if xi is None else xi + xi), None))
            continue
        yr, yi = spec[n // 2 - k]
        even.append((plus(xr, yr), minus(xi, yi)))
        dr, di = minus(xr, yr), plus(xi, yi)
        odd.append(turn(dr, di, -k, n))
    even[0], odd[0] = (even[0][0], None), (odd[0][0], None)
    first, second = real_inverse(even, n // 2), real_inverse(odd, n // 2)
    return [v for pair in zip(first, second) for v in pair]


def make_tables(w, wi, twist):
    tokens = w.shape[0] // 2
    tiles = twist.shape[0] - 1
    j = lax.broadcasted_iota(jnp.int32, (tokens, tokens), 0)
    k = lax.broadcasted_iota(jnp.int32, (tokens, tokens), 1)
    phase = lax.rem(j * k, tokens).astype(jnp.float32) * (2.0 * math.pi / tokens)
    cb, sb = jnp.cos(phase).astype(jnp.bfloat16), jnp.sin(phase).astype(jnp.bfloat16)
    for ref, sign in ((w, -1.0), (wi, 1.0)):
        ref[0:tokens, 0:tokens] = cb
        ref[tokens : 2 * tokens, tokens : 2 * tokens] = cb
        ref[0:tokens, tokens : 2 * tokens] = sb * sign
        ref[tokens : 2 * tokens, 0:tokens] = sb * -sign
    lane = lax.broadcasted_iota(jnp.int32, (1, tokens), 1)
    unit = 2.0 * math.pi / (2 * tiles * tokens)

    def row(t, carry):
        angle = (lane * t).astype(jnp.float32) * unit
        twist[t, 0:1, :] = jnp.cos(angle)
        twist[t, 1:2, :] = jnp.sin(angle)
        return carry

    lax.fori_loop(0, tiles + 1, row, 0)


ROWS = 16
VMEM_MIB = 49


def transform(rx, out, w, wi, twist, spec, back):
    _, tiles, rows, tokens = rx.shape
    full = 2 * tiles * tokens
    shrink = 1.0 / math.sqrt(tiles * tokens)
    steps = rows // ROWS

    def first(t, carry):
        s, i = lax.div(t, steps), lax.rem(t, steps)
        at = pl.ds(pl.multiple_of(i * ROWS, ROWS), ROWS)
        x = [rx[s, a, at, :].astype(jnp.float32) for a in range(tiles)]
        for k, (re, im) in enumerate(real_dft(x, 2 * tiles)):
            if k == 0:
                new_re, new_im = re, jnp.zeros_like(re)
            else:
                c, d = twist[k, 0:1, :], twist[k, 1:2, :]
                new_re = plus(re * c, None if im is None else im * d)
                new_im = minus(None if im is None else im * c, re * d)
            spec[s, k, at, 0:tokens] = new_re.astype(jnp.bfloat16)
            spec[s, k, at, tokens : 2 * tokens] = new_im.astype(jnp.bfloat16)
        return carry

    lax.fori_loop(0, 3 * steps, first, 0)

    def middle(k, carry):
        def spectrum(s):
            u = jnp.dot(spec[s, k], w[...], preferred_element_type=jnp.float32)
            u = u.astype(jnp.bfloat16).astype(jnp.float32)
            return u[:, :tokens], u[:, tokens:]

        hr, hi = spectrum(0)
        zr, zi = spectrum(1)
        dr, di = spectrum(2)
        c = twist[k, 0:1, :] * (1.0 / full)
        d = twist[k, 1:2, :] * (1.0 / full)
        for s, (ur, ui, f) in enumerate(((hr, hi, 1.0), (zr, zi, shrink))):
            qr = ur * dr + ui * di
            qi = ur * di - ui * dr
            if s:
                qr, qi = qr * f, qi * f
            q = jnp.concatenate([qr, qi], axis=1).astype(jnp.bfloat16)
            e = jnp.dot(q, wi[...], preferred_element_type=jnp.float32)
            er, ei = e[:, :tokens], e[:, tokens:]
            back[s, k, :, 0:tokens] = (er * c - ei * d).astype(jnp.bfloat16)
            back[s, k, :, tokens : 2 * tokens] = (er * d + ei * c).astype(jnp.bfloat16)
        return carry

    lax.fori_loop(0, tiles + 1, middle, 0)

    def last(t, carry):
        s, i = lax.div(t, steps), lax.rem(t, steps)
        at = pl.ds(pl.multiple_of(i * ROWS, ROWS), ROWS)
        pieces = []
        for k in range(tiles + 1):
            re = back[s, k, at, 0:tokens].astype(jnp.float32)
            im = None
            if 0 < k < tiles:
                im = back[s, k, at, tokens : 2 * tokens].astype(jnp.float32)
            pieces.append((re, im))
        for a, value in enumerate(real_inverse(pieces, 2 * tiles)):
            out[s, a, at, :] = value.astype(jnp.bfloat16)
        return carry

    lax.fori_loop(0, 2 * steps, last, 0)


MESH = pl.DeviceIdType.MESH


def kernel(
    n, sections, group,
    arriving, taps, gate_in, inner_src, vals_src, saved_src, bias,
    gate_out, inner_out, vals_out, taps_out,
    gate, inner_in, vals, saved, w, wi, twist,
    grad, stage, rx, res, q, biased, spec, back,
    loads, pair_send, pair_recv, send, recv, home, back_send, back_recv, back_home,
):
    me, sec = lax.axis_index("ctx"), lax.axis_index("pipe")
    groups = arriving.shape[1] // group

    def rows_of(g):
        return pl.ds(pl.multiple_of(g * group, group), group)

    def peer_of(d):
        return lax.rem(me + d, n)

    def load(i):
        src = (inner_src, vals_src, gate_in, saved_src)[i]
        dst = (inner_in, vals, gate, saved)[i]
        return pltpu.make_async_copy(src, dst, loads.at[i])

    for i in range(4):
        load(i).start()
    barrier = pltpu.get_barrier_semaphore()
    pl.semaphore_signal(
        barrier, inc=1, device_id={"pipe": lax.rem(sec + 1, sections)}, device_id_type=MESH
    )

    def greet(d, carry):
        pl.semaphore_signal(barrier, inc=1, device_id={"ctx": peer_of(d)}, device_id_type=MESH)
        return carry

    lax.fori_loop(1, n, greet, 0)
    pl.semaphore_wait(barrier, n)

    def pair(g):
        return pltpu.make_async_remote_copy(
            src_ref=arriving.at[:, rows_of(g)],
            dst_ref=grad.at[:, rows_of(g)],
            send_sem=pair_send.at[g],
            recv_sem=pair_recv.at[g],
            device_id={"pipe": lax.rem(sec + sections - 1, sections)},
            device_id_type=MESH,
        )

    def start_pair(g, carry):
        pair(g).start()
        return carry

    lax.fori_loop(0, groups, start_pair, 0)

    def ship(src, g, s, p):
        pltpu.make_async_remote_copy(
            src_ref=src,
            dst_ref=rx.at[g, s, me],
            send_sem=send.at[g],
            recv_sem=recv.at[g],
            device_id={"ctx": p},
            device_id_type=MESH,
        ).start()

    def own_taps(g):
        return pltpu.make_async_copy(taps.at[me, rows_of(g)], rx.at[g, 0, me], home.at[g])

    def post_taps(g):
        def send_taps(d, c):
            ship(taps.at[peer_of(d), rows_of(g)], g, 0, peer_of(d))
            return c

        lax.fori_loop(1, n, send_taps, 0)
        own_taps(g).start()

    def forward(g, carry):
        rows = rows_of(g)

        def product(left, right, s):
            def one(p):
                return (left[p, rows].astype(jnp.float32) * right[p, rows].astype(jnp.float32)).astype(
                    jnp.bfloat16
                )

            def make(d, c):
                stage[g, s - 1, peer_of(d)] = one(peer_of(d))
                return c

            lax.fori_loop(1, n, make, 0)
            rx[g, s, me] = one(me)

            def post(d, c):
                ship(stage.at[g, s - 1, peer_of(d)], g, s, peer_of(d))
                return c

            lax.fori_loop(1, n, post, 0)

        product(inner_in, vals, 1)
        pair(g).wait_recv()
        product(grad, gate, 2)

        @pl.when(g + 1 < groups)
        def _():
            post_taps(g + 1)

        return carry

    post_taps(0)
    for i in range(3):
        load(i).wait()
    lax.fori_loop(0, groups, forward, 0)
    load(3).wait()
    make_tables(w, wi, twist)
    own, tokens = arriving.shape[1:]
    lanes = 128
    f32 = jnp.float32

    def side(b, carry):
        if own >= lanes:
            per = own // lanes
            at = (lax.div(b, per), pl.ds(pl.multiple_of(lax.rem(b, per) * lanes, lanes), lanes))
        else:
            at = (pl.ds(b * (lanes // own), lanes // own),)
        shape = grad[at].shape
        g = grad[at].astype(f32).reshape(lanes, tokens)
        gate_out[at] = (g * saved[at].astype(f32).reshape(lanes, tokens)).astype(
            jnp.bfloat16
        ).reshape(shape)
        d_out = (g * gate[at].astype(f32).reshape(lanes, tokens)).astype(jnp.bfloat16)
        row = bias[:, pl.ds(pl.multiple_of(b * lanes, lanes), lanes)]
        column = jnp.transpose(jnp.broadcast_to(row, (tokens, lanes)))
        biased[at] = (column * d_out.astype(f32)).reshape(shape)
        return carry

    lax.fori_loop(0, n * own // lanes, side, 0)

    def own_result(g):
        return pltpu.make_async_copy(
            res.at[g, :, me], q.at[g, :, me], back_home.at[g]
        )

    def turn_group(g, carry):
        landed = rx.at[g, :, pl.ds(0, n - 1)]
        pltpu.make_async_copy(landed, landed, recv.at[g]).wait()
        own_taps(g).wait()
        transform(rx.at[g], res.at[g], w, wi, twist, spec, back)

        def reply(d, c):
            pltpu.make_async_remote_copy(
                src_ref=res.at[g, :, peer_of(d)],
                dst_ref=q.at[g, :, me],
                send_sem=back_send.at[g],
                recv_sem=back_recv.at[g],
                device_id={"ctx": peer_of(d)},
                device_id_type=MESH,
            ).start()
            return c

        lax.fori_loop(1, n, reply, 0)
        own_result(g).start()
        return carry

    lax.fori_loop(0, groups, turn_group, 0)

    def finish(g, carry):
        rows = rows_of(g)
        replies = q.at[g, :, pl.ds(0, n - 1)]
        pltpu.make_async_copy(replies, replies, back_recv.at[g]).wait()
        own_result(g).wait()

        def product(p, c):
            dz = q[g, 0, p].astype(f32) + biased[p, rows]
            inner_out[p, rows] = (dz * vals[p, rows].astype(f32)).astype(jnp.bfloat16)
            vals_out[p, rows] = (dz * inner_in[p, rows].astype(f32)).astype(jnp.bfloat16)
            taps_out[p, rows] = q[g, 1, p]
            return c

        lax.fori_loop(0, n, product, 0)
        pair(g).wait_send()
        sent = rx.at[g, :, pl.ds(0, n - 1)]
        pltpu.make_async_copy(sent, sent, send.at[g]).wait()
        replied = res.at[g, :, pl.ds(0, n - 1)]
        pltpu.make_async_copy(replied, replied, back_send.at[g]).wait()
        return carry

    lax.fori_loop(0, groups, finish, 0)


def exchange(arriving, taps, gate, inner_in, vals, saved, bias, n, sections):
    _, own, tokens = arriving.shape
    group = max(ROWS, own // 4)
    groups = own // group
    bf16 = jnp.bfloat16
    vmem = pl.BlockSpec(memory_space=pltpu.VMEM)
    hbm = pl.BlockSpec(memory_space=pltpu.HBM)
    dma = pltpu.SemaphoreType.DMA
    whole = jax.ShapeDtypeStruct((n, own, tokens), bf16)
    held = pltpu.VMEM((n, own, tokens), bf16)
    return pl.pallas_call(
        functools.partial(kernel, n, sections, group),
        in_specs=[hbm] * 6 + [vmem],
        out_specs=[vmem] * 4,
        out_shape=[whole] * 4,
        scratch_shapes=[
            held, held, held, held,
            pltpu.VMEM((2 * tokens, 2 * tokens), bf16),
            pltpu.VMEM((2 * tokens, 2 * tokens), bf16),
            pltpu.VMEM((n + 1, 2, tokens), jnp.float32),
            held,
            pltpu.VMEM((groups, 2, n, group, tokens), bf16),
            pltpu.VMEM((groups, 3, n, group, tokens), bf16),
            pltpu.VMEM((groups, 2, n, group, tokens), bf16),
            pltpu.VMEM((groups, 2, n, group, tokens), bf16),
            pltpu.VMEM((n, own, tokens), jnp.float32),
            pltpu.VMEM((3, n + 1, group, 2 * tokens), bf16),
            pltpu.VMEM((2, n + 1, group, 2 * tokens), bf16),
            dma((4,)),
            dma((groups,)), dma((groups,)), dma((groups,)), dma((groups,)), dma((groups,)),
            dma((groups,)), dma((groups,)), dma((groups,)),
        ],
        compiler_params=pltpu.CompilerParams(
            collective_id=0, has_side_effects=True, vmem_limit_bytes=VMEM_MIB * 2**20
        ),
    )(arriving, taps, gate, inner_in, vals, saved, bias)


def write_out(a, b, c, narrow, a_out, b_out, c_out, wide_out, wide, sems):
    n = narrow.shape[0]
    part = max(1, n // 4)
    plain = [
        pltpu.make_async_copy(src, dst, sems.at[i])
        for i, (src, dst) in enumerate(((a, a_out), (b, b_out), (c, c_out)))
    ]
    for copy in plain:
        copy.start()
    widened = []
    for i in range(n // part):

        def widen(p, carry):
            wide[p] = narrow[p].astype(jnp.float32)
            return carry

        lax.fori_loop(i * part, (i + 1) * part, widen, 0)
        at = pl.ds(i * part, part)
        copy = pltpu.make_async_copy(wide.at[at], wide_out.at[at], sems.at[3 + i])
        copy.start()
        widened.append(copy)
    for copy in plain + widened:
        copy.wait()


def finish_outputs(d_gate, inner_gradient, d_values, d_filters):
    shape = d_gate.shape
    vmem = pl.BlockSpec(memory_space=pltpu.VMEM)
    hbm = pl.BlockSpec(memory_space=pl.ANY)
    narrow = jax.ShapeDtypeStruct(shape, jnp.bfloat16)
    return pl.pallas_call(
        write_out,
        in_specs=[vmem] * 4,
        out_specs=[hbm] * 4,
        out_shape=[narrow] * 3 + [jax.ShapeDtypeStruct(shape, jnp.float32)],
        scratch_shapes=[
            pltpu.VMEM(shape, jnp.float32),
            pltpu.SemaphoreType.DMA((3 + shape[0] // max(1, shape[0] // 4),)),
        ],
        compiler_params=pltpu.CompilerParams(vmem_limit_bytes=VMEM_MIB * 2**20),
    )(d_gate, inner_gradient, d_values, d_filters)


def per_device(arriving, input_gate, input_inner, values, conv_out, filters, bias):
    tiles = lax.axis_size("ctx")
    sections = lax.axis_size("pipe")
    channels, tokens = values.shape[1:]
    own = channels // tiles

    def split(array):
        return array[0].reshape(tiles, own, tokens)

    outs = exchange(
        split(arriving), split(filters), split(input_gate), split(input_inner), split(values),
        split(conv_out), bias, tiles, sections,
    )
    return tuple(array.reshape(1, channels, tokens) for array in finish_outputs(*outs))


def solution(mesh):
    spread = P("pipe", None, "ctx")
    return jax.shard_map(
        per_device,
        mesh=mesh,
        in_specs=(spread,) * 6 + (P("pipe", None),),
        out_specs=(spread,) * 4,
        check_vma=False,
    )
```

profile of v0, /device:TPU:0, one launch (start us, length us, event | category | flops | bytes accessed | tf_op | source)
XLA Modules:
  0.0 120.5 jit_solution(2070246161304546867)
XLA Ops:
  0.6 0.0 copy-start
  0.6 0.7 copy-done
  1.4 116.7 %shard_map.102 = (bf16[16,256,128]{2,1,0:T(8,128)(2,1)S(1)}, bf16[16,256,128]{2,1,0:T(8,128)(2,1)S(1)}, bf16[16,256,128]{2,1,0:T(8,128)(2,1)S(1)}, bf16[16,256,128]{2,1,0:T(8,128)(2,1)S(1)}) custom-call(bf16[16,256,128]{2,1,0:T(8,128)(2,1)} %bitcast.10, bf16[16,256,128]{2,1,0:T(8,128)(2,1)} %bitcast.11, bf16[16,256,128]{2,1,0:T(8,128)(2,1)} %bitcast.12, ...), custom_call_target="tpu_custom_call" | custom-call | tf_op jit(solution)/shard_map/pallas_call | solution.py:365
  118.1 2.4 %shard_map.103 = (bf16[16,256,128]{2,1,0:T(8,128)(2,1)}, bf16[16,256,128]{2,1,0:T(8,128)(2,1)}, bf16[16,256,128]{2,1,0:T(8,128)(2,1)}, f32[16,256,128]{2,1,0:T(8,128)}) custom-call(bf16[16,256,128]{2,1,0:T(8,128)(2,1)S(1)} %get-tuple-element.12.a, bf16[16,256,128]{2,1,0:T(8,128)(2,1)S(1)} %get-tuple-element.13.b, ...), custom_call_target="tpu_custom_call" | custom-call | tf_op jit(solution)/shard_map/pallas_call | solution.py:423
Async XLA Ops:
  0.6 0.7 copy-start
where the time goes:
time: 123 us; the launch traced here: 120 us
  Pallas kernels  119 us (97%)
    pallas_call x1, Pallas kernels, exchange(): pl.pallas_call(functools.partial(kernel, n, sections, group), in_specs=[h...  117 us

commit v1 on v0

v1 whole, which is shorter than its diff:
```python
import functools
import math

import jax
import jax.numpy as jnp
from jax import lax
from jax.experimental import pallas as pl
from jax.experimental.pallas import tpu as pltpu
from jax.sharding import PartitionSpec as P


def plus(a, b):
    return b if a is None else a if b is None else a + b


def minus(a, b):
    return a if b is None else -b if a is None else a - b


def turn(a, b, k, n):
    k = k % n
    if k == 0:
        return a, b
    if 4 * k == n:
        return b, minus(None, a)
    if 4 * k == 3 * n:
        return minus(None, b), a
    c, s = math.cos(2 * math.pi * k / n), math.sin(2 * math.pi * k / n)

    def scaled(v, f):
        return None if v is None else v * f

    if 8 * k == n:
        return scaled(plus(a, b), c), scaled(minus(b, a), c)
    return plus(scaled(a, c), scaled(b, s)), minus(scaled(b, c), scaled(a, s))


def real_dft(x, n):
    if n == 2:
        return [(x[0], None), (x[0], None)]
    even, odd = real_dft(x[0::2], n // 2), real_dft(x[1::2], n // 2)
    out = [None] * (n // 2 + 1)
    for k in range(n // 4 + 1):
        er, ei = even[k]
        tr, ti = turn(*odd[k], k, n)
        if 4 * k == n:
            out[k] = (plus(er, tr), plus(ei, ti))
        else:
            out[k] = (plus(er, tr), plus(ei, ti))
            out[n // 2 - k] = (minus(er, tr), minus(ti, ei))
    return out


def real_inverse(spec, n):
    if n == 2:
        return [plus(spec[0][0], spec[1][0])]
    even, odd = [], []
    for k in range(n // 4 + 1):
        xr, xi = spec[k]
        if 4 * k == n:
            even.append((xr + xr, None))
            odd.append((minus(None, None if xi is None else xi + xi), None))
            continue
        yr, yi = spec[n // 2 - k]
        even.append((plus(xr, yr), minus(xi, yi)))
        dr, di = minus(xr, yr), plus(xi, yi)
        odd.append(turn(dr, di, -k, n))
    even[0], odd[0] = (even[0][0], None), (odd[0][0], None)
    first, second = real_inverse(even, n // 2), real_inverse(odd, n // 2)
    return [v for pair in zip(first, second) for v in pair]


def make_tables(w, wi, twist):
    tokens = w.shape[0] // 2
    tiles = twist.shape[0] - 1
    j = lax.broadcasted_iota(jnp.int32, (tokens, tokens), 0)
    k = lax.broadcasted_iota(jnp.int32, (tokens, tokens), 1)
    phase = lax.rem(j * k, tokens).astype(jnp.float32) * (2.0 * math.pi / tokens)
    cb, sb = jnp.cos(phase).astype(jnp.bfloat16), jnp.sin(phase).astype(jnp.bfloat16)
    for ref, sign in ((w, -1.0), (wi, 1.0)):
        ref[0:tokens, 0:tokens] = cb
        ref[tokens : 2 * tokens, tokens : 2 * tokens] = cb
        ref[0:tokens, tokens : 2 * tokens] = sb * sign
        ref[tokens : 2 * tokens, 0:tokens] = sb * -sign
    lane = lax.broadcasted_iota(jnp.int32, (1, tokens), 1)
    unit = 2.0 * math.pi / (2 * tiles * tokens)

    def row(t, carry):
        angle = (lane * t).astype(jnp.float32) * unit
        twist[t, 0:1, :] = jnp.cos(angle)
        twist[t, 1:2, :] = jnp.sin(angle)
        return carry

    lax.fori_loop(0, tiles + 1, row, 0)


CH = 16
GROUP = 4
LAG = 14
LATE = 6
VMEM_MIB = 56
MESH = pl.DeviceIdType.MESH
f32, bf16 = jnp.float32, jnp.bfloat16


def correlate(x_at, d_at, put, first_d, tiles, whole, stride, w, wi, twist, spec, freq):
    tokens = w.shape[0] // 2
    bins = tiles + 1
    full = 2 * tiles * tokens
    shrink = 1.0 / math.sqrt(whole * tokens)
    rows = bins * CH

    def block(k):
        return slice(k * CH, (k + 1) * CH)

    for s in range(3):
        if s < 2:
            x = [x_at(s, a).astype(f32) for a in range(tiles)]
        else:
            x = [None if a < first_d else d_at(a - first_d).astype(f32) for a in range(tiles)]
        for k, (re, im) in enumerate(real_dft(x, 2 * tiles)):
            if k == 0:
                new_re, new_im = re, jnp.zeros_like(re)
            else:
                c, d = twist[k * stride, 0:1, :], twist[k * stride, 1:2, :]
                new_re = plus(re * c, None if im is None else im * d)
                new_im = minus(None if im is None else im * c, re * d)
            spec[s, block(k), 0:tokens] = new_re.astype(bf16)
            spec[s, block(k), tokens : 2 * tokens] = new_im.astype(bf16)
    for s in range(3):
        freq[s, 0:rows] = jnp.dot(spec[s, 0:rows], w[...], preferred_element_type=f32)
    for k in range(bins):
        dr, di = freq[2, block(k), 0:tokens], freq[2, block(k), tokens : 2 * tokens]
        for s in range(2):
            ur, ui = freq[s, block(k), 0:tokens], freq[s, block(k), tokens : 2 * tokens]
            spec[s, block(k), 0:tokens] = (ur * dr + ui * di).astype(bf16)
            spec[s, block(k), tokens : 2 * tokens] = (ur * di - ui * dr).astype(bf16)
    for s in range(2):
        freq[s, 0:rows] = jnp.dot(spec[s, 0:rows], wi[...], preferred_element_type=f32)
    for s, scale in enumerate((1.0 / full, shrink / full)):
        pieces = []
        for k in range(bins):
            er, ei = freq[s, block(k), 0:tokens], freq[s, block(k), tokens : 2 * tokens]
            c, d = twist[k * stride, 0:1, :] * scale, twist[k * stride, 1:2, :] * scale
            pieces.append((er * c - ei * d, (er * d + ei * c) if 0 < k < tiles else None))
        for a, value in enumerate(real_inverse(pieces, 2 * tiles)):
            put(s, a, value.astype(bf16))


def wait_for(ref, sem):
    pltpu.make_async_copy(ref, ref, sem).wait()


def each(count, body):
    def step(i, carry):
        body(i)
        return carry

    lax.fori_loop(0, count, step, 0)


def kernel(
    n, sections,
    arriving, taps, gate_in, inner_src, vals_src, saved_src, bias,
    gate_out, inner_out, vals_out, taps_out,
    gate, inner_in, vals, saved, grad, inner, d_out, biased,
    rx, rd, upper, out, mine,
    w, wi, twist, spec, freq,
    loads, home, pair_send, pair_recv, swap_send,
    x_in, d_in, x_rel, d_rel, low_in, up_in, mine_in,
    rel_send, low_send, up_send, out_send,
):
    me, sec = lax.axis_index("ctx"), lax.axis_index("pipe")
    side, chunks, _, tokens = arriving.shape
    half = 2 * side
    plane, column = lax.div(me, side), lax.rem(me, side)
    groups = chunks // GROUP
    pieces = pair_recv.shape[0]
    start = lax.div(me, half) * half
    lag = min(LAG, chunks)
    relays = (plane == 0) | (plane == 3)

    sources = (inner_src, vals_src, gate_in, saved_src)
    copies = [
        pltpu.make_async_copy(src, dst, loads.at[i])
        for i, (src, dst) in enumerate(zip(sources, (inner_in, vals, gate, saved)))
    ]
    for copy in copies:
        copy.start()

    barrier = pltpu.get_barrier_semaphore()

    def greet(peer):
        pl.semaphore_signal(barrier, inc=1, device_id={"ctx": peer}, device_id_type=MESH)

    pl.semaphore_signal(
        barrier, inc=1, device_id={"pipe": lax.rem(sec + 1, sections)}, device_id_type=MESH
    )
    each(half - 1, lambda d: greet(start + lax.rem(me - start + 1 + d, half)))

    @pl.when(jnp.logical_not(relays))
    def _():
        greet((3 - plane) * side + column)
        make_tables(w, wi, twist)
        pl.semaphore_wait(barrier, half + 1)

    @pl.when(relays)
    def _():
        pl.semaphore_wait(barrier, half)

    part = chunks // pieces

    def pair(p):
        at = pl.ds(p * part, part)
        return pltpu.make_async_remote_copy(
            src_ref=arriving.at[:, at],
            dst_ref=grad.at[:, at],
            send_sem=pair_send.at[p],
            recv_sem=pair_recv.at[p],
            device_id={"pipe": lax.rem(sec + sections - 1, sections)},
            device_id_type=MESH,
        )

    for p in range(pieces):
        pair(p).start()

    def chunk_range(g):
        return pl.ds(pl.multiple_of(g * GROUP, GROUP), GROUP)

    def send(src, dst, sent, received, peer):
        pltpu.make_async_remote_copy(
            src_ref=src, dst_ref=dst, send_sem=sent, recv_sem=received,
            device_id={"ctx": peer}, device_id_type=MESH,
        ).start()

    def others(body):
        each(side - 1, lambda d: body(lax.rem(column + 1 + d, side)))

    def own_taps(g):
        at = chunk_range(g)
        return pltpu.make_async_copy(taps.at[column, at], rx.at[at, 0, me], home.at[g])

    for copy in copies[:3]:
        copy.wait()

    def swap(g):
        at = chunk_range(g)
        base = plane * side

        def product(left, right, u):
            return (left[u, at].astype(f32) * right[u, at].astype(f32)).astype(bf16)

        own_taps(g).start()

        def first(u):
            send(taps.at[u, at], rx.at[at, 0, me], swap_send.at[0], x_in.at[g], base + u)
            inner[u, at] = product(inner_in, vals, u)

        others(first)
        rx[at, 1, me] = product(inner_in, vals, column)

        def second(u):
            send(inner.at[u, at], rx.at[at, 1, me], swap_send.at[1], x_in.at[g], base + u)

        others(second)

        @pl.when(lax.rem(g * GROUP, part) == 0)
        def _():
            pair(lax.div(g * GROUP, part)).wait_recv()

        def third(u):
            d_out[u, at] = product(grad, gate, u)

        others(third)
        own = product(grad, gate, column)
        d_out[column, at] = own
        rd[at, me - start] = own

        def fourth(u):
            send(d_out.at[u, at], rd.at[at, me - start], swap_send.at[2], d_in.at[g], base + u)

        others(fourth)

    each(groups, swap)
    copies[3].wait()
    lanes = 8 * CH

    def beside(j):
        def one(u):
            at = (u, pl.ds(pl.multiple_of(j * 8, 8), 8))
            shape = (8, CH, tokens)
            gate_out[at] = (grad[at].astype(f32) * saved[at].astype(f32)).astype(bf16)
            lane = pl.multiple_of((u * (chunks // 8) + j) * lanes, lanes)
            row = bias[:, pl.ds(lane, lanes)]
            tall = jnp.transpose(jnp.broadcast_to(row, (tokens, lanes)))
            biased[at] = tall.reshape(shape) * d_out[at].astype(f32)

        each(side, one)

    def finish(g):
        at = chunk_range(g)

        @pl.when(relays)
        def _():
            wait_for(mine.at[:, pl.ds(0, GROUP)], mine_in.at[g])

        @pl.when(jnp.logical_not(relays))
        def _():
            wait_for(mine.at[pl.ds(0, side - 1), pl.ds(0, GROUP)], mine_in.at[g])

        def one(u):
            dz = mine[u, at, 0].astype(f32) + biased[u, at]
            inner_out[u, at] = (dz * vals[u, at].astype(f32)).astype(bf16)
            vals_out[u, at] = (dz * inner_in[u, at].astype(f32)).astype(bf16)
            taps_out[u, at] = mine[u, at, 1]

        each(side, one)

    def own_plane_in(g):
        wait_for(rx.at[pl.ds(0, GROUP), :, pl.ds(0, side - 1)], x_in.at[g])
        own_taps(g).wait()

    def d_plane_in(g):
        wait_for(rd.at[pl.ds(0, GROUP), pl.ds(0, side - 1)], d_in.at[g])

    def landed(g):
        own_plane_in(g)
        wait_for(rx.at[pl.ds(0, GROUP), :, pl.ds(0, side)], x_rel.at[g])
        d_plane_in(g)
        wait_for(rd.at[pl.ds(0, GROUP), pl.ds(0, side)], d_rel.at[g])

    def to_owners(k):
        def one(d):
            t = start + lax.rem(me - start + 1 + d, half)
            send(out.at[k, :, t], mine.at[column, k], out_send, mine_in.at[lax.div(k, GROUP)], t)

        each(half - 1, one)
        mine[column, k] = out[k, :, me]

    def finish_at(k):
        late = chunks // 2

        @pl.when((k >= late) & (lax.rem(k, 2) == 0))
        def _():
            g = lax.div(k - late, 2)

            @pl.when((g + 1) * GROUP + LATE <= k)
            def _():
                finish(g)

    def finished(last):
        late = chunks // 2
        return sum(1 for k in range(late, last) if k % 2 == 0 and ((k - late) // 2 + 1) * GROUP + LATE <= k)

    tables = (w, wi, twist, spec, freq)

    def values_of(k):
        def x_at(s, a):
            return rx[k, s, a]

        def d_at(a):
            return rd[k, a]

        def put(s, a, value):
            out[k, s, a] = value

        return x_at, d_at, put

    @pl.when(relays)
    def _():
        target = lax.select(plane == 0, side + column, half + column)
        tiles = pl.ds(plane * side, side)
        half_tiles = pl.ds(plane * side - start, side)

        def relay(g):
            at = chunk_range(g)
            own_plane_in(g)
            send(rx.at[at, :, tiles], rx.at[at, :, tiles], rel_send.at[0], x_rel.at[g], target)
            d_plane_in(g)
            send(rd.at[at, half_tiles], rd.at[at, half_tiles], rel_send.at[1], d_rel.at[g], target)

        each(groups, relay)
        each(chunks // 8, beside)
        each(groups, finish)
        wait_for(rx.at[:, :, pl.ds(0, side)], rel_send.at[0])
        wait_for(rd.at[:, pl.ds(0, side)], rel_send.at[1])

    @pl.when(plane == 1)
    def _():
        low = pl.ds(0, half)

        def step(k):
            @pl.when(k < chunks)
            def _():
                @pl.when(lax.rem(k, GROUP) == 0)
                def _():
                    landed(lax.div(k, GROUP))

                    def forward(i):
                        send(
                            rx.at[k + i, :, low], rx.at[k + i, :, low],
                            low_send, low_in.at[k + i], half + column,
                        )

                    each(GROUP, forward)

                correlate(*values_of(k), 0, half, n, 2, *tables)

                @pl.when(lax.rem(k, 8) == 0)
                def _():
                    beside(lax.div(k, 8))

            @pl.when(k >= lag)
            def _():
                i = k - lag
                wait_for(upper.at[i], up_in.at[i])

                def add(s):
                    out[i, s, low] = (
                        out[i, s, low].astype(f32) + upper[i, s].astype(f32)
                    ).astype(bf16)

                each(2, add)
                to_owners(i)
                finish_at(i)

        each(chunks + lag, step)
        done = finished(chunks)
        each(groups - done, lambda i: finish(done + i))
        wait_for(rx.at[:, :, low], low_send)
        wait_for(out.at[:, :, pl.ds(0, half - 1)], out_send)

    @pl.when(plane == 2)
    def _():
        low = pl.ds(0, half)

        def step(k):
            @pl.when(lax.rem(k, GROUP) == 0)
            def _():
                landed(lax.div(k, GROUP))

            wait_for(rx.at[k, :, low], low_in.at[k])
            correlate(*values_of(k), half, n, n, 1, *tables)
            send(out.at[k, :, low], upper.at[k], up_send, up_in.at[k], side + column)
            to_owners(k)

            @pl.when(lax.rem(k, 8) == 0)
            def _():
                beside(lax.div(k, 8))

            finish_at(k)

        each(chunks, step)
        done = finished(chunks)
        each(groups - done, lambda i: finish(done + i))
        wait_for(out.at[:, :, low], up_send)
        wait_for(out.at[:, :, pl.ds(0, half - 1)], out_send)

    for p in range(pieces):
        pair(p).wait_send()
    for i in range(3):
        wait_for(inner.at[pl.ds(0, side - 1)], swap_send.at[i])


def exchange(arriving, taps, gate, inner_in, vals, saved, bias, n, sections):
    side, chunks, _, tokens = arriving.shape
    half = 2 * side
    groups = chunks // GROUP
    vmem = pl.BlockSpec(memory_space=pltpu.VMEM)
    hbm = pl.BlockSpec(memory_space=pltpu.HBM)
    dma = pltpu.SemaphoreType.DMA
    shape = (side, chunks, CH, tokens)
    held = pltpu.VMEM(shape, bf16)
    rows = (n + 1) * CH
    pieces = max(1, min(4, groups))
    return pl.pallas_call(
        functools.partial(kernel, n, sections),
        in_specs=[hbm] * 6 + [vmem],
        out_specs=[vmem] * 4,
        out_shape=[jax.ShapeDtypeStruct(shape, bf16)] * 4,
        scratch_shapes=[
            held, held, held, held, held, held, held,
            pltpu.VMEM(shape, f32),
            pltpu.VMEM((chunks, 2, n, CH, tokens), bf16),
            pltpu.VMEM((chunks, half, CH, tokens), bf16),
            pltpu.VMEM((chunks, 2, half, CH, tokens), bf16),
            pltpu.VMEM((chunks, 2, n, CH, tokens), bf16),
            pltpu.VMEM((side, chunks, 2, CH, tokens), bf16),
            pltpu.VMEM((2 * tokens, 2 * tokens), bf16),
            pltpu.VMEM((2 * tokens, 2 * tokens), bf16),
            pltpu.VMEM((n + 1, 2, tokens), f32),
            pltpu.VMEM((3, rows, 2 * tokens), bf16),
            pltpu.VMEM((3, rows, 2 * tokens), f32),
            dma((4,)), dma((groups,)), dma((pieces,)), dma((pieces,)), dma((3,)),
            dma((groups,)), dma((groups,)), dma((groups,)), dma((groups,)),
            dma((chunks,)), dma((chunks,)), dma((groups,)),
            dma((2,)), dma, dma, dma,
        ],
        compiler_params=pltpu.CompilerParams(
            collective_id=0, has_side_effects=True, vmem_limit_bytes=VMEM_MIB * 2**20
        ),
    )(arriving, taps, gate, inner_in, vals, saved, bias)


def write_out(a, b, c, narrow, a_out, b_out, c_out, wide_out, wide, sems):
    n = narrow.shape[0]
    part = max(1, n // 4)
    plain = [
        pltpu.make_async_copy(src, dst, sems.at[i])
        for i, (src, dst) in enumerate(((a, a_out), (b, b_out), (c, c_out)))
    ]
    for copy in plain:
        copy.start()
    widened = []
    for i in range(n // part):

        def widen(p, carry):
            wide[p] = narrow[p].astype(jnp.float32)
            return carry

        lax.fori_loop(i * part, (i + 1) * part, widen, 0)
        at = pl.ds(i * part, part)
        copy = pltpu.make_async_copy(wide.at[at], wide_out.at[at], sems.at[3 + i])
        copy.start()
        widened.append(copy)
    for copy in plain + widened:
        copy.wait()


def finish_outputs(d_gate, inner_gradient, d_values, d_filters):
    shape = d_gate.shape
    vmem = pl.BlockSpec(memory_space=pltpu.VMEM)
    hbm = pl.BlockSpec(memory_space=pl.ANY)
    narrow = jax.ShapeDtypeStruct(shape, jnp.bfloat16)
    return pl.pallas_call(
        write_out,
        in_specs=[vmem] * 4,
        out_specs=[hbm] * 4,
        out_shape=[narrow] * 3 + [jax.ShapeDtypeStruct(shape, jnp.float32)],
        scratch_shapes=[
            pltpu.VMEM(shape, jnp.float32),
            pltpu.SemaphoreType.DMA((3 + shape[0] // max(1, shape[0] // 4),)),
        ],
        compiler_params=pltpu.CompilerParams(vmem_limit_bytes=VMEM_MIB * 2**20),
    )(d_gate, inner_gradient, d_values, d_filters)


def per_device(arriving, input_gate, input_inner, values, conv_out, filters, bias):
    tiles = lax.axis_size("ctx")
    sections = lax.axis_size("pipe")
    channels, tokens = values.shape[1:]
    side = tiles // 4

    def split(array):
        return array[0].reshape(side, channels // (side * CH), CH, tokens)

    outs = exchange(
        split(arriving), split(filters), split(input_gate), split(input_inner), split(values),
        split(conv_out), bias, tiles, sections,
    )
    return tuple(array.reshape(1, channels, tokens) for array in finish_outputs(*outs))


def solution(mesh):
    spread = P("pipe", None, "ctx")
    return jax.shard_map(
        per_device,
        mesh=mesh,
        in_specs=(spread,) * 6 + (P("pipe", None),),
        out_specs=(spread,) * 4,
        check_vma=False,
    )
```

time: 123 us -> 125 us (1.016); the launches traced: 120 us -> 125 us
  Pallas kernels: 119 us -> 124 us
    pallas_call x1, Pallas kernels: 117 us -> 120 us  [exchange(): pl.pallas_call(functools.partial(kernel, n, sections), in_specs=[hbm] * 6...]
    pallas_call x1, Pallas kernels: 2.39 us -> 4.57 us  [finish_outputs(): pl.pallas_call(write_out, in_specs=[vmem] * 4, out_specs=[hbm] * 4, out_s...]
where the time goes in v1:
time: 125 us
  Pallas kernels  124 us (99%)
    pallas_call x1, Pallas kernels, exchange(): pl.pallas_call(functools.partial(kernel, n, sections), in_specs=[hbm] * 6...  120 us
    pallas_call x1, Pallas kernels, finish_outputs(): pl.pallas_call(write_out, in_specs=[vmem] * 4, out_specs=[hbm] * 4, out_s...  4.57 us

profile of v1, /device:TPU:0, one launch (start us, length us, event | category | flops | bytes accessed | tf_op | source)
XLA Modules:
  0.0 124.8 jit_solution(5991023323498077286)
XLA Ops:
  0.6 119.5 %shard_map.102 = (bf16[4,64,16,128]{3,2,1,0:T(8,128)(2,1)}, bf16[4,64,16,128]{3,2,1,0:T(8,128)(2,1)}, bf16[4,64,16,128]{3,2,1,0:T(8,128)(2,1)}, bf16[4,64,16,128]{3,2,1,0:T(8,128)(2,1)}) custom-call(bf16[4,64,16,128]{3,2,1,0:T(8,128)(2,1)} %bitcast.10, bf16[4,64,16,128]{3,2,1,0:T(8,128)(2,1)} %bitcast.11, bf16[4,64,16,128]{3,2,1,0:T(8,128)(2,1)} %bitcast.12, ...), custom_call_target="tpu_custom_call" | custom-call | tf_op jit(solution)/shard_map/pallas_call | solution.py:476
  120.2 4.6 %shard_map.103 = (bf16[4,64,16,128]{3,2,1,0:T(8,128)(2,1)}, bf16[4,64,16,128]{3,2,1,0:T(8,128)(2,1)}, bf16[4,64,16,128]{3,2,1,0:T(8,128)(2,1)}, f32[4,64,16,128]{3,2,1,0:T(8,128)}) custom-call(bf16[4,64,16,128]{3,2,1,0:T(8,128)(2,1)} %get-tuple-element.12.a, bf16[4,64,16,128]{3,2,1,0:T(8,128)(2,1)} %get-tuple-element.13.b, ...), custom_call_target="tpu_custom_call" | custom-call | tf_op jit(solution)/shard_map/pallas_call | solution.py:535

commit v2 on v1

--- a/solution.py
+++ b/solution.py
@@ -96,9 +96,10 @@
 
 CH = 16
 GROUP = 4
+AHEAD = 2
 LAG = 14
-LATE = 6
-VMEM_MIB = 56
+LATE = 8
+VMEM_MIB = 49
 MESH = pl.DeviceIdType.MESH
 f32, bf16 = jnp.float32, jnp.bfloat16
 
@@ -159,11 +160,15 @@
     lax.fori_loop(0, count, step, 0)
 
 
+def pair_edges(chunks):
+    return sorted({0, GROUP, max(GROUP, chunks // 4), max(GROUP, chunks // 2), chunks})
+
+
 def kernel(
     n, sections,
-    arriving, taps, gate_in, inner_src, vals_src, saved_src, bias,
+    arriving, taps, gate_in, inner_src, vals_src, saved_src, bias_src,
     gate_out, inner_out, vals_out, taps_out,
-    gate, inner_in, vals, saved, grad, inner, d_out, biased,
+    gate, inner_in, vals, saved, bias, grad, inner, d_out, biased,
     rx, rd, upper, out, mine,
     w, wi, twist, spec, freq,
     loads, home, pair_send, pair_recv, swap_send,
@@ -175,15 +180,16 @@
     half = 2 * side
     plane, column = lax.div(me, side), lax.rem(me, side)
     groups = chunks // GROUP
-    pieces = pair_recv.shape[0]
     start = lax.div(me, half) * half
+    base = plane * side
     lag = min(LAG, chunks)
     relays = (plane == 0) | (plane == 3)
-
-    sources = (inner_src, vals_src, gate_in, saved_src)
+    low = pl.ds(0, half)
+
+    sources = (inner_src, vals_src, gate_in, saved_src, bias_src)
     copies = [
         pltpu.make_async_copy(src, dst, loads.at[i])
-        for i, (src, dst) in enumerate(zip(sources, (inner_in, vals, gate, saved)))
+        for i, (src, dst) in enumerate(zip(sources, (inner_in, vals, gate, saved, bias)))
     ]
     for copy in copies:
         copy.start()
@@ -193,25 +199,35 @@
     def greet(peer):
         pl.semaphore_signal(barrier, inc=1, device_id={"ctx": peer}, device_id_type=MESH)
 
+    def others(body):
+        each(side - 1, lambda d: body(lax.rem(column + 1 + d, side)))
+
     pl.semaphore_signal(
         barrier, inc=1, device_id={"pipe": lax.rem(sec + 1, sections)}, device_id_type=MESH
     )
-    each(half - 1, lambda d: greet(start + lax.rem(me - start + 1 + d, half)))
+    others(lambda u: greet(base + u))
+
+    @pl.when(plane > 0)
+    def _():
+        greet(me - side)
+
+    @pl.when(plane < 3)
+    def _():
+        greet(me + side)
 
     @pl.when(jnp.logical_not(relays))
     def _():
-        greet((3 - plane) * side + column)
         make_tables(w, wi, twist)
-        pl.semaphore_wait(barrier, half + 1)
+        pl.semaphore_wait(barrier, side + 2)
 
     @pl.when(relays)
     def _():
-        pl.semaphore_wait(barrier, half)
-
-    part = chunks // pieces
+        pl.semaphore_wait(barrier, side + 1)
+
+    edges = pair_edges(chunks)
 
     def pair(p):
-        at = pl.ds(p * part, part)
+        at = pl.ds(edges[p], edges[p + 1] - edges[p])
         return pltpu.make_async_remote_copy(
             src_ref=arriving.at[:, at],
             dst_ref=grad.at[:, at],
@@ -221,11 +237,8 @@
             device_id_type=MESH,
         )
 
-    for p in range(pieces):
+    for p in range(len(edges) - 1):
         pair(p).start()
-
-    def chunk_range(g):
-        return pl.ds(pl.multiple_of(g * GROUP, GROUP), GROUP)
 
     def send(src, dst, sent, received, peer):
         pltpu.make_async_remote_copy(
@@ -233,40 +246,37 @@
             device_id={"ctx": peer}, device_id_type=MESH,
         ).start()
 
-    def others(body):
-        each(side - 1, lambda d: body(lax.rem(column + 1 + d, side)))
-
-    def own_taps(g):
-        at = chunk_range(g)
-        return pltpu.make_async_copy(taps.at[column, at], rx.at[at, 0, me], home.at[g])
+    def own_taps(k, size, unit):
+        at = pl.ds(k, size)
+        return pltpu.make_async_copy(taps.at[column, at], rx.at[at, 0, me], home.at[unit])
 
     for copy in copies[:3]:
         copy.wait()
 
-    def swap(g):
-        at = chunk_range(g)
-        base = plane * side
+    def swap(k, size, unit):
+        at = pl.ds(k, size)
 
         def product(left, right, u):
             return (left[u, at].astype(f32) * right[u, at].astype(f32)).astype(bf16)
 
-        own_taps(g).start()
+        own_taps(k, size, unit).start()
 
         def first(u):
-            send(taps.at[u, at], rx.at[at, 0, me], swap_send.at[0], x_in.at[g], base + u)
+            send(taps.at[u, at], rx.at[at, 0, me], swap_send.at[0], x_in.at[unit], base + u)
             inner[u, at] = product(inner_in, vals, u)
 
         others(first)
         rx[at, 1, me] = product(inner_in, vals, column)
 
         def second(u):
-            send(inner.at[u, at], rx.at[at, 1, me], swap_send.at[1], x_in.at[g], base + u)
+            send(inner.at[u, at], rx.at[at, 1, me], swap_send.at[1], x_in.at[unit], base + u)
 
         others(second)
-
-        @pl.when(lax.rem(g * GROUP, part) == 0)
-        def _():
-            pair(lax.div(g * GROUP, part)).wait_recv()
+        for p in range(len(edges) - 1):
+
+            @pl.when(k == edges[p])
+            def _():
+                pair(p).wait_recv()
 
         def third(u):
             d_out[u, at] = product(grad, gate, u)
@@ -277,12 +287,35 @@
         rd[at, me - start] = own
 
         def fourth(u):
-            send(d_out.at[u, at], rd.at[at, me - start], swap_send.at[2], d_in.at[g], base + u)
+            send(d_out.at[u, at], rd.at[at, me - start], swap_send.at[2], d_in.at[unit], base + u)
 
         others(fourth)
 
-    each(groups, swap)
-    copies[3].wait()
+    def swap_group(g):
+        swap(pl.multiple_of(g * GROUP, GROUP), GROUP, GROUP - 1 + g)
+
+    def swap_next(g):
+        @pl.when(g + AHEAD + 1 < groups)
+        def _():
+            swap_group(g + AHEAD + 1)
+
+    def at_unit(k, body):
+        @pl.when(k < GROUP)
+        def _():
+            body(k, 1, k)
+
+        @pl.when((k >= GROUP) & (lax.rem(k, GROUP) == 0))
+        def _():
+            body(pl.multiple_of(k, GROUP), GROUP, GROUP - 1 + lax.div(k, GROUP))
+
+        @pl.when(lax.rem(k, GROUP) == 0)
+        def _():
+            swap_next(lax.div(k, GROUP))
+
+    each(GROUP, lambda k: swap(k, 1, k))
+    each(min(AHEAD, groups - 1), lambda g: swap_group(g + 1))
+    for copy in copies[3:]:
+        copy.wait()
     lanes = 8 * CH
 
     def beside(j):
@@ -297,8 +330,13 @@
 
         each(side, one)
 
+    def beside_at(k):
+        @pl.when(lax.rem(k, 8) == 4)
+        def _():
+            beside(lax.div(k, 8))
+
     def finish(g):
-        at = chunk_range(g)
+        at = pl.ds(pl.multiple_of(g * GROUP, GROUP), GROUP)
 
         @pl.when(relays)
         def _():
@@ -316,18 +354,29 @@
 
         each(side, one)
 
-    def own_plane_in(g):
-        wait_for(rx.at[pl.ds(0, GROUP), :, pl.ds(0, side - 1)], x_in.at[g])
-        own_taps(g).wait()
-
-    def d_plane_in(g):
-        wait_for(rd.at[pl.ds(0, GROUP), pl.ds(0, side - 1)], d_in.at[g])
-
-    def landed(g):
-        own_plane_in(g)
-        wait_for(rx.at[pl.ds(0, GROUP), :, pl.ds(0, side)], x_rel.at[g])
-        d_plane_in(g)
-        wait_for(rd.at[pl.ds(0, GROUP), pl.ds(0, side)], d_rel.at[g])
+    def finish_at(k):
+        g = lax.div(k - LATE, GROUP) - 1
+
+        @pl.when((k >= LATE + GROUP) & (lax.rem(k - LATE, GROUP) == 0))
+        def _():
+            finish(g)
+
+    def finish_rest():
+        done = max(0, (chunks - 1 - LATE) // GROUP)
+        each(groups - done, lambda i: finish(done + i))
+
+    def x_plane_in(k, size, unit):
+        wait_for(rx.at[pl.ds(0, size), :, pl.ds(0, side - 1)], x_in.at[unit])
+        own_taps(k, size, unit).wait()
+
+    def d_plane_in(size, unit):
+        wait_for(rd.at[pl.ds(0, size), pl.ds(0, side - 1)], d_in.at[unit])
+
+    def x_relayed(size, unit):
+        wait_for(rx.at[pl.ds(0, size), :, pl.ds(0, side)], x_rel.at[unit])
+
+    def d_relayed(size, unit):
+        wait_for(rd.at[pl.ds(0, size), pl.ds(0, side)], d_rel.at[unit])
 
     def to_owners(k):
         def one(d):
@@ -337,21 +386,6 @@
         each(half - 1, one)
         mine[column, k] = out[k, :, me]
 
-    def finish_at(k):
-        late = chunks // 2
-
-        @pl.when((k >= late) & (lax.rem(k, 2) == 0))
-        def _():
-            g = lax.div(k - late, 2)
-
-            @pl.when((g + 1) * GROUP + LATE <= k)
-            def _():
-                finish(g)
-
-    def finished(last):
-        late = chunks // 2
-        return sum(1 for k in range(late, last) if k % 2 == 0 and ((k - late) // 2 + 1) * GROUP + LATE <= k)
-
     tables = (w, wi, twist, spec, freq)
 
     def values_of(k):
@@ -369,17 +403,17 @@
     @pl.when(relays)
     def _():
         target = lax.select(plane == 0, side + column, half + column)
-        tiles = pl.ds(plane * side, side)
-        half_tiles = pl.ds(plane * side - start, side)
-
-        def relay(g):
-            at = chunk_range(g)
-            own_plane_in(g)
-            send(rx.at[at, :, tiles], rx.at[at, :, tiles], rel_send.at[0], x_rel.at[g], target)
-            d_plane_in(g)
-            send(rd.at[at, half_tiles], rd.at[at, half_tiles], rel_send.at[1], d_rel.at[g], target)
-
-        each(groups, relay)
+        tiles = pl.ds(base, side)
+        half_tiles = pl.ds(base - start, side)
+
+        def relay(k, size, unit):
+            at = pl.ds(k, size)
+            x_plane_in(k, size, unit)
+            send(rx.at[at, :, tiles], rx.at[at, :, tiles], rel_send.at[0], x_rel.at[unit], target)
+            d_plane_in(size, unit)
+            send(rd.at[at, half_tiles], rd.at[at, half_tiles], rel_send.at[1], d_rel.at[unit], target)
+
+        each(chunks, lambda k: at_unit(k, relay))
         each(chunks // 8, beside)
         each(groups, finish)
         wait_for(rx.at[:, :, pl.ds(0, side)], rel_send.at[0])
@@ -387,28 +421,26 @@
 
     @pl.when(plane == 1)
     def _():
-        low = pl.ds(0, half)
+        def arrive(k, size, unit):
+            x_plane_in(k, size, unit)
+            x_relayed(size, unit)
+
+            def forward(i):
+                send(
+                    rx.at[k + i, :, low], rx.at[k + i, :, low],
+                    low_send, low_in.at[k + i], half + column,
+                )
+
+            each(size, forward)
+            d_plane_in(size, unit)
+            d_relayed(size, unit)
 
         def step(k):
             @pl.when(k < chunks)
             def _():
-                @pl.when(lax.rem(k, GROUP) == 0)
-                def _():
-                    landed(lax.div(k, GROUP))
-
-                    def forward(i):
-                        send(
-                            rx.at[k + i, :, low], rx.at[k + i, :, low],
-                            low_send, low_in.at[k + i], half + column,
-                        )
-
-                    each(GROUP, forward)
-
+                at_unit(k, arrive)
                 correlate(*values_of(k), 0, half, n, 2, *tables)
-
-                @pl.when(lax.rem(k, 8) == 0)
-                def _():
-                    beside(lax.div(k, 8))
+                beside_at(k)
 
             @pl.when(k >= lag)
             def _():
@@ -425,38 +457,33 @@
                 finish_at(i)
 
         each(chunks + lag, step)
-        done = finished(chunks)
-        each(groups - done, lambda i: finish(done + i))
+        finish_rest()
         wait_for(rx.at[:, :, low], low_send)
         wait_for(out.at[:, :, pl.ds(0, half - 1)], out_send)
 
     @pl.when(plane == 2)
     def _():
-        low = pl.ds(0, half)
+        def arrive(k, size, unit):
+            x_plane_in(k, size, unit)
+            x_relayed(size, unit)
+            d_plane_in(size, unit)
+            d_relayed(size, unit)
 
         def step(k):
-            @pl.when(lax.rem(k, GROUP) == 0)
-            def _():
-                landed(lax.div(k, GROUP))
-
+            at_unit(k, arrive)
             wait_for(rx.at[k, :, low], low_in.at[k])
             correlate(*values_of(k), half, n, n, 1, *tables)
             send(out.at[k, :, low], upper.at[k], up_send, up_in.at[k], side + column)
             to_owners(k)
-
-            @pl.when(lax.rem(k, 8) == 0)
-            def _():
-                beside(lax.div(k, 8))
-
+            beside_at(k)
             finish_at(k)
 
         each(chunks, step)
-        done = finished(chunks)
-        each(groups - done, lambda i: finish(done + i))
+        finish_rest()
         wait_for(out.at[:, :, low], up_send)
         wait_for(out.at[:, :, pl.ds(0, half - 1)], out_send)
 
-    for p in range(pieces):
+    for p in range(len(edges) - 1):
         pair(p).wait_send()
     for i in range(3):
         wait_for(inner.at[pl.ds(0, side - 1)], swap_send.at[i])
@@ -466,20 +493,24 @@
     side, chunks, _, tokens = arriving.shape
     half = 2 * side
     groups = chunks // GROUP
+    units = GROUP - 1 + groups
+    pieces = len(pair_edges(chunks)) - 1
     vmem = pl.BlockSpec(memory_space=pltpu.VMEM)
     hbm = pl.BlockSpec(memory_space=pltpu.HBM)
     dma = pltpu.SemaphoreType.DMA
     shape = (side, chunks, CH, tokens)
     held = pltpu.VMEM(shape, bf16)
     rows = (n + 1) * CH
-    pieces = max(1, min(4, groups))
+    limit = max(VMEM_MIB, 48 + n // 16) * 2**20
     return pl.pallas_call(
         functools.partial(kernel, n, sections),
-        in_specs=[hbm] * 6 + [vmem],
+        in_specs=[hbm] * 7,
         out_specs=[vmem] * 4,
         out_shape=[jax.ShapeDtypeStruct(shape, bf16)] * 4,
         scratch_shapes=[
-            held, held, held, held, held, held, held,
+            held, held, held, held,
+            pltpu.VMEM(bias.shape, f32),
+            held, held, held,
             pltpu.VMEM(shape, f32),
             pltpu.VMEM((chunks, 2, n, CH, tokens), bf16),
             pltpu.VMEM((chunks, half, CH, tokens), bf16),
@@ -491,13 +522,13 @@
             pltpu.VMEM((n + 1, 2, tokens), f32),
             pltpu.VMEM((3, rows, 2 * tokens), bf16),
             pltpu.VMEM((3, rows, 2 * tokens), f32),
-            dma((4,)), dma((groups,)), dma((pieces,)), dma((pieces,)), dma((3,)),
-            dma((groups,)), dma((groups,)), dma((groups,)), dma((groups,)),
+            dma((5,)), dma((units,)), dma((pieces,)), dma((pieces,)), dma((3,)),
+            dma((units,)), dma((units,)), dma((units,)), dma((units,)),
             dma((chunks,)), dma((chunks,)), dma((groups,)),
             dma((2,)), dma, dma, dma,
         ],
         compiler_params=pltpu.CompilerParams(
-            collective_id=0, has_side_effects=True, vmem_limit_bytes=VMEM_MIB * 2**20
+            collective_id=0, has_side_effects=True, vmem_limit_bytes=limit
         ),
     )(arriving, taps, gate, inner_in, vals, saved, bias)
 

time: 125 us -> 117 us (0.936)
  Pallas kernels: 124 us -> 115 us
    pallas_call x1, Pallas kernels: 120 us -> 113 us  [exchange(): pl.pallas_call(functools.partial(kernel, n, sections), in_specs=[hbm] * 7...]
    pallas_call x1, Pallas kernels: 4.57 us -> 2.39 us  [finish_outputs(): pl.pallas_call(write_out, in_specs=[vmem] * 4, out_specs=[hbm] * 4, out_s...]
where the time goes in v2:
time: 117 us
  Pallas kernels  115 us (98%)
    pallas_call x1, Pallas kernels, exchange(): pl.pallas_call(functools.partial(kernel, n, sections), in_specs=[hbm] * 7...  113 us
    pallas_call x1, Pallas kernels, finish_outputs(): pl.pallas_call(write_out, in_specs=[vmem] * 4, out_specs=[hbm] * 4, out_s...  2.39 us

profile of v2, /device:TPU:0, one launch (start us, length us, event | category | flops | bytes accessed | tf_op | source)
XLA Modules:
  0.0 116.8 jit_solution(10628155625588520551)
XLA Ops:
  0.6 0.0 copy-start
  0.6 0.7 copy-done
  1.4 113.1 %shard_map.102 = (bf16[4,64,16,128]{3,2,1,0:T(8,128)(2,1)S(1)}, bf16[4,64,16,128]{3,2,1,0:T(8,128)(2,1)S(1)}, bf16[4,64,16,128]{3,2,1,0:T(8,128)(2,1)S(1)}, bf16[4,64,16,128]{3,2,1,0:T(8,128)(2,1)S(1)}) custom-call(bf16[4,64,16,128]{3,2,1,0:T(8,128)(2,1)} %bitcast.10, bf16[4,64,16,128]{3,2,1,0:T(8,128)(2,1)} %bitcast.11, bf16[4,64,16,128]{3,2,1,0:T(8,128)(2,1)} %bitcast.12, ...), custom_call_target="tpu_custom_call" | custom-call | tf_op jit(solution)/shard_map/pallas_call | solution.py:505
  114.4 2.4 %shard_map.103 = (bf16[4,64,16,128]{3,2,1,0:T(8,128)(2,1)}, bf16[4,64,16,128]{3,2,1,0:T(8,128)(2,1)}, bf16[4,64,16,128]{3,2,1,0:T(8,128)(2,1)}, f32[4,64,16,128]{3,2,1,0:T(8,128)}) custom-call(bf16[4,64,16,128]{3,2,1,0:T(8,128)(2,1)S(1)} %get-tuple-element.12.a, bf16[4,64,16,128]{3,2,1,0:T(8,128)(2,1)S(1)} %get-tuple-element.13.b, ...), custom_call_target="tpu_custom_call" | custom-call | tf_op jit(solution)/shard_map/pallas_call | solution.py:566
Async XLA Ops:
  0.6 0.7 copy-start

commit v3 on v2

--- a/solution.py
+++ b/solution.py
@@ -96,8 +96,8 @@
 
 CH = 16
 GROUP = 4
-AHEAD = 2
-LAG = 14
+AHEAD = 3
+LAG = 8
 LATE = 8
 VMEM_MIB = 49
 MESH = pl.DeviceIdType.MESH
@@ -169,11 +169,11 @@
     arriving, taps, gate_in, inner_src, vals_src, saved_src, bias_src,
     gate_out, inner_out, vals_out, taps_out,
     gate, inner_in, vals, saved, bias, grad, inner, d_out, biased,
-    rx, rd, upper, out, mine,
+    rx, rd, upper, out, mine, ends,
     w, wi, twist, spec, freq,
     loads, home, pair_send, pair_recv, swap_send,
     x_in, d_in, x_rel, d_rel, low_in, up_in, mine_in,
-    rel_send, low_send, up_send, out_send,
+    ends_in, rel_send, low_send, up_send, out_send, ends_send,
 ):
     me, sec = lax.axis_index("ctx"), lax.axis_index("pipe")
     side, chunks, _, tokens = arriving.shape
@@ -218,6 +218,7 @@
     @pl.when(jnp.logical_not(relays))
     def _():
         make_tables(w, wi, twist)
+
         pl.semaphore_wait(barrier, side + 2)
 
     @pl.when(relays)
@@ -237,8 +238,7 @@
             device_id_type=MESH,
         )
 
-    for p in range(len(edges) - 1):
-        pair(p).start()
+    pair(0).start()
 
     def send(src, dst, sent, received, peer):
         pltpu.make_async_remote_copy(
@@ -253,25 +253,27 @@
     for copy in copies[:3]:
         copy.wait()
 
-    def swap(k, size, unit):
+    def product(left, right, u, at):
+        return (left[u, at].astype(f32) * right[u, at].astype(f32)).astype(bf16)
+
+    def swap_x(k, size, unit):
         at = pl.ds(k, size)
-
-        def product(left, right, u):
-            return (left[u, at].astype(f32) * right[u, at].astype(f32)).astype(bf16)
-
         own_taps(k, size, unit).start()
 
         def first(u):
             send(taps.at[u, at], rx.at[at, 0, me], swap_send.at[0], x_in.at[unit], base + u)
-            inner[u, at] = product(inner_in, vals, u)
+            inner[u, at] = product(inner_in, vals, u, at)
 
         others(first)
-        rx[at, 1, me] = product(inner_in, vals, column)
+        rx[at, 1, me] = product(inner_in, vals, column, at)
 
         def second(u):
             send(inner.at[u, at], rx.at[at, 1, me], swap_send.at[1], x_in.at[unit], base + u)
 
         others(second)
+
+    def swap_d(k, size, unit):
+        at = pl.ds(k, size)
         for p in range(len(edges) - 1):
 
             @pl.when(k == edges[p])
@@ -279,10 +281,10 @@
                 pair(p).wait_recv()
 
         def third(u):
-            d_out[u, at] = product(grad, gate, u)
+            d_out[u, at] = product(grad, gate, u, at)
 
         others(third)
-        own = product(grad, gate, column)
+        own = product(grad, gate, column, at)
         d_out[column, at] = own
         rd[at, me - start] = own
 
@@ -291,15 +293,22 @@
 
         others(fourth)
 
-    def swap_group(g):
-        swap(pl.multiple_of(g * GROUP, GROUP), GROUP, GROUP - 1 + g)
-
     def swap_next(g):
-        @pl.when(g + AHEAD + 1 < groups)
-        def _():
-            swap_group(g + AHEAD + 1)
+        @pl.when(g < groups)
+        def _():
+            k, unit = pl.multiple_of(g * GROUP, GROUP), GROUP - 1 + g
+            swap_x(k, GROUP, unit)
+            swap_d(k, GROUP, unit)
 
     def at_unit(k, body):
+        @pl.when(k < AHEAD)
+        def _():
+            swap_next(k + 1)
+
+        @pl.when((k >= GROUP) & (lax.rem(k, GROUP) == 0))
+        def _():
+            swap_next(lax.div(k, GROUP) + AHEAD)
+
         @pl.when(k < GROUP)
         def _():
             body(k, 1, k)
@@ -308,12 +317,10 @@
         def _():
             body(pl.multiple_of(k, GROUP), GROUP, GROUP - 1 + lax.div(k, GROUP))
 
-        @pl.when(lax.rem(k, GROUP) == 0)
-        def _():
-            swap_next(lax.div(k, GROUP))
-
-    each(GROUP, lambda k: swap(k, 1, k))
-    each(min(AHEAD, groups - 1), lambda g: swap_group(g + 1))
+    each(GROUP, lambda k: swap_x(k, 1, k))
+    each(GROUP, lambda k: swap_d(k, 1, k))
+    for p in range(1, len(edges) - 1):
+        pair(p).start()
     for copy in copies[3:]:
         copy.wait()
     lanes = 8 * CH
@@ -335,7 +342,7 @@
         def _():
             beside(lax.div(k, 8))
 
-    def finish(g):
+    def finish(g, extra=None):
         at = pl.ds(pl.multiple_of(g * GROUP, GROUP), GROUP)
 
         @pl.when(relays)
@@ -348,9 +355,12 @@
 
         def one(u):
             dz = mine[u, at, 0].astype(f32) + biased[u, at]
+            dh = mine[u, at, 1].astype(f32)
+            if extra is not None:
+                dz, dh = dz + extra[u, :, 0].astype(f32), dh + extra[u, :, 1].astype(f32)
             inner_out[u, at] = (dz * vals[u, at].astype(f32)).astype(bf16)
             vals_out[u, at] = (dz * inner_in[u, at].astype(f32)).astype(bf16)
-            taps_out[u, at] = mine[u, at, 1]
+            taps_out[u, at] = dh.astype(bf16)
 
         each(side, one)
 
@@ -363,7 +373,18 @@
 
     def finish_rest():
         done = max(0, (chunks - 1 - LATE) // GROUP)
-        each(groups - done, lambda i: finish(done + i))
+        each(groups - 1 - done, lambda i: finish(done + i))
+        finish_last()
+
+    def finish_last():
+        @pl.when(start > 0)
+        def _():
+            finish(groups - 1)
+
+        @pl.when(start == 0)
+        def _():
+            wait_for(ends, ends_in)
+            finish(groups - 1, ends)
 
     def x_plane_in(k, size, unit):
         wait_for(rx.at[pl.ds(0, size), :, pl.ds(0, side - 1)], x_in.at[unit])
@@ -415,7 +436,9 @@
 
         each(chunks, lambda k: at_unit(k, relay))
         each(chunks // 8, beside)
-        each(groups, finish)
+        each(groups - 1, finish)
+        finish_last()
+
         wait_for(rx.at[:, :, pl.ds(0, side)], rel_send.at[0])
         wait_for(rd.at[:, pl.ds(0, side)], rel_send.at[1])
 
@@ -445,14 +468,18 @@
             @pl.when(k >= lag)
             def _():
                 i = k - lag
-                wait_for(upper.at[i], up_in.at[i])
-
-                def add(s):
-                    out[i, s, low] = (
-                        out[i, s, low].astype(f32) + upper[i, s].astype(f32)
-                    ).astype(bf16)
-
-                each(2, add)
+
+                @pl.when(i < chunks - GROUP)
+                def _():
+                    wait_for(upper.at[i], up_in.at[i])
+
+                    def add(s):
+                        out[i, s, low] = (
+                            out[i, s, low].astype(f32) + upper[i, s].astype(f32)
+                        ).astype(bf16)
+
+                    each(2, add)
+
                 to_owners(i)
                 finish_at(i)
 
@@ -473,14 +500,29 @@
             at_unit(k, arrive)
             wait_for(rx.at[k, :, low], low_in.at[k])
             correlate(*values_of(k), half, n, n, 1, *tables)
-            send(out.at[k, :, low], upper.at[k], up_send, up_in.at[k], side + column)
+
+            @pl.when(k < chunks - GROUP)
+            def _():
+                send(out.at[k, :, low], upper.at[k], up_send, up_in.at[k], side + column)
+
+            @pl.when(k >= chunks - GROUP)
+            def _():
+                def last(t):
+                    send(
+                        out.at[k, :, t], ends.at[column, k - (chunks - GROUP)],
+                        ends_send, ends_in, t,
+                    )
+
+                each(half, last)
+
             to_owners(k)
             beside_at(k)
             finish_at(k)
 
         each(chunks, step)
         finish_rest()
-        wait_for(out.at[:, :, low], up_send)
+        wait_for(out.at[pl.ds(0, chunks - GROUP), :, low], up_send)
+        wait_for(out.at[pl.ds(0, GROUP), :, low], ends_send)
         wait_for(out.at[:, :, pl.ds(0, half - 1)], out_send)
 
     for p in range(len(edges) - 1):
@@ -501,7 +543,7 @@
     shape = (side, chunks, CH, tokens)
     held = pltpu.VMEM(shape, bf16)
     rows = (n + 1) * CH
-    limit = max(VMEM_MIB, 48 + n // 16) * 2**20
+    limit = max(VMEM_MIB, 48 + n * 10 // 128) * 2**20
     return pl.pallas_call(
         functools.partial(kernel, n, sections),
         in_specs=[hbm] * 7,
@@ -517,6 +559,7 @@
             pltpu.VMEM((chunks, 2, half, CH, tokens), bf16),
             pltpu.VMEM((chunks, 2, n, CH, tokens), bf16),
             pltpu.VMEM((side, chunks, 2, CH, tokens), bf16),
+            pltpu.VMEM((side, GROUP, 2, CH, tokens), bf16),
             pltpu.VMEM((2 * tokens, 2 * tokens), bf16),
             pltpu.VMEM((2 * tokens, 2 * tokens), bf16),
             pltpu.VMEM((n + 1, 2, tokens), f32),
@@ -525,7 +568,7 @@
             dma((5,)), dma((units,)), dma((pieces,)), dma((pieces,)), dma((3,)),
             dma((units,)), dma((units,)), dma((units,)), dma((units,)),
             dma((chunks,)), dma((chunks,)), dma((groups,)),
-            dma((2,)), dma, dma, dma,
+            dma, dma((2,)), dma, dma, dma, dma,
         ],
         compiler_params=pltpu.CompilerParams(
             collective_id=0, has_side_effects=True, vmem_limit_bytes=limit

time: 117 us -> 116 us (level)
    pallas_call x1, Pallas kernels: 113 us -> 112 us  [exchange(): pl.pallas_call(functools.partial(kernel, n, sections), in_specs=[hbm] * 7...]
where the time goes in v3:
time: 116 us; the launch traced here: 115 us
  Pallas kernels  114 us (98%)
    pallas_call x1, Pallas kernels, exchange(): pl.pallas_call(functools.partial(kernel, n, sections), in_specs=[hbm] * 7...  112 us
    pallas_call x1, Pallas kernels, finish_outputs(): pl.pallas_call(write_out, in_specs=[vmem] * 4, out_specs=[hbm] * 4, out_s...  2.39 us

profile of v3, /device:TPU:0, one launch (start us, length us, event | category | flops | bytes accessed | tf_op | source)
XLA Modules:
  0.0 115.3 jit_solution(2444820382287595394)
XLA Ops:
  0.6 0.0 copy-start
  0.6 0.7 copy-done
  1.4 111.5 %shard_map.102 = (bf16[4,64,16,128]{3,2,1,0:T(8,128)(2,1)S(1)}, bf16[4,64,16,128]{3,2,1,0:T(8,128)(2,1)S(1)}, bf16[4,64,16,128]{3,2,1,0:T(8,128)(2,1)S(1)}, bf16[4,64,16,128]{3,2,1,0:T(8,128)(2,1)S(1)}) custom-call(bf16[4,64,16,128]{3,2,1,0:T(8,128)(2,1)} %bitcast.10, bf16[4,64,16,128]{3,2,1,0:T(8,128)(2,1)} %bitcast.11, bf16[4,64,16,128]{3,2,1,0:T(8,128)(2,1)} %bitcast.12, ...), custom_call_target="tpu_custom_call" | custom-call | tf_op jit(solution)/shard_map/pallas_call | solution.py:547
  112.9 2.4 %shard_map.103 = (bf16[4,64,16,128]{3,2,1,0:T(8,128)(2,1)}, bf16[4,64,16,128]{3,2,1,0:T(8,128)(2,1)}, bf16[4,64,16,128]{3,2,1,0:T(8,128)(2,1)}, f32[4,64,16,128]{3,2,1,0:T(8,128)}) custom-call(bf16[4,64,16,128]{3,2,1,0:T(8,128)(2,1)S(1)} %get-tuple-element.12.a, bf16[4,64,16,128]{3,2,1,0:T(8,128)(2,1)S(1)} %get-tuple-element.13.b, ...), custom_call_target="tpu_custom_call" | custom-call | tf_op jit(solution)/shard_map/pallas_call | solution.py:609
Async XLA Ops:
  0.6 0.7 copy-start

commit v4 on v3

--- a/solution.py
+++ b/solution.py
@@ -98,7 +98,6 @@
 GROUP = 4
 AHEAD = 3
 LAG = 8
-LATE = 8
 VMEM_MIB = 49
 MESH = pl.DeviceIdType.MESH
 f32, bf16 = jnp.float32, jnp.bfloat16
@@ -183,6 +182,8 @@
     start = lax.div(me, half) * half
     base = plane * side
     lag = min(LAG, chunks)
+    first_beside = max(chunks // 4 + 2, chunks // 2 - 12)
+    late = max(2 * GROUP, first_beside - 2)
     relays = (plane == 0) | (plane == 3)
     low = pl.ds(0, half)
 
@@ -338,9 +339,11 @@
         each(side, one)
 
     def beside_at(k):
-        @pl.when(lax.rem(k, 8) == 4)
-        def _():
-            beside(lax.div(k, 8))
+        j = k - first_beside
+
+        @pl.when((j >= 0) & (j < chunks // 2) & (lax.rem(j, 4) == 0))
+        def _():
+            beside(lax.div(j, 4))
 
     def finish(g, extra=None):
         at = pl.ds(pl.multiple_of(g * GROUP, GROUP), GROUP)
@@ -365,14 +368,14 @@
         each(side, one)
 
     def finish_at(k):
-        g = lax.div(k - LATE, GROUP) - 1
-
-        @pl.when((k >= LATE + GROUP) & (lax.rem(k - LATE, GROUP) == 0))
+        g = lax.div(k - late, GROUP) - 1
+
+        @pl.when((k >= late + GROUP) & (lax.rem(k - late, GROUP) == 0))
         def _():
             finish(g)
 
     def finish_rest():
-        done = max(0, (chunks - 1 - LATE) // GROUP)
+        done = max(0, (chunks - 1 - late) // GROUP)
         each(groups - 1 - done, lambda i: finish(done + i))
         finish_last()
 

time: 116 us -> 115 us (level)
  no operation moved by 1% of the time
where the time goes in v4:
time: 115 us
  Pallas kernels  113 us (98%)
    pallas_call x1, Pallas kernels, exchange(): pl.pallas_call(functools.partial(kernel, n, sections), in_specs=[hbm] * 7...  111 us
    pallas_call x1, Pallas kernels, finish_outputs(): pl.pallas_call(write_out, in_specs=[vmem] * 4, out_specs=[hbm] * 4, out_s...  2.39 us

profile of v4, /device:TPU:0, one launch (start us, length us, event | category | flops | bytes accessed | tf_op | source)
XLA Modules:
  0.0 114.8 jit_solution(2539070896167028726)
XLA Ops:
  0.6 0.0 copy-start
  0.6 0.7 copy-done
  1.4 111.0 %shard_map.102 = (bf16[4,64,16,128]{3,2,1,0:T(8,128)(2,1)S(1)}, bf16[4,64,16,128]{3,2,1,0:T(8,128)(2,1)S(1)}, bf16[4,64,16,128]{3,2,1,0:T(8,128)(2,1)S(1)}, bf16[4,64,16,128]{3,2,1,0:T(8,128)(2,1)S(1)}) custom-call(bf16[4,64,16,128]{3,2,1,0:T(8,128)(2,1)} %bitcast.10, bf16[4,64,16,128]{3,2,1,0:T(8,128)(2,1)} %bitcast.11, bf16[4,64,16,128]{3,2,1,0:T(8,128)(2,1)} %bitcast.12, ...), custom_call_target="tpu_custom_call" | custom-call | tf_op jit(solution)/shard_map/pallas_call | solution.py:550
  112.4 2.4 %shard_map.103 = (bf16[4,64,16,128]{3,2,1,0:T(8,128)(2,1)}, bf16[4,64,16,128]{3,2,1,0:T(8,128)(2,1)}, bf16[4,64,16,128]{3,2,1,0:T(8,128)(2,1)}, f32[4,64,16,128]{3,2,1,0:T(8,128)}) custom-call(bf16[4,64,16,128]{3,2,1,0:T(8,128)(2,1)S(1)} %get-tuple-element.12.a, bf16[4,64,16,128]{3,2,1,0:T(8,128)(2,1)S(1)} %get-tuple-element.13.b, ...), custom_call_target="tpu_custom_call" | custom-call | tf_op jit(solution)/shard_map/pallas_call | solution.py:612
Async XLA Ops:
  0.6 0.7 copy-start
